TPU v7x, 32 devices: a whole 2x2x4 slice. The times are simulated.
32 devices in a mesh: dp: 4 (over z), seq: 2 (over core), tensor: 4 (over y, x).
Axes of the slice: x: 2, y: 2, z: 4, core: 2. Of those that a mesh axis runs over, the one named last changes fastest.
Arguments:
- block_input: bfloat16 [1024, 1024], P(('dp', 'seq')), may hold values from -6 to 6
- norm1_gain: float32 [1024], replicated, may hold values from 0.5 to 1.5
- q_weight: bfloat16 [1024, 768], replicated, may hold values from -0.1875 to 0.1875
- k_weight: bfloat16 [1024, 768], replicated, may hold values from -0.1875 to 0.1875
- v_weight: bfloat16 [1024, 6, 256], P(None, None, 'tensor'), may hold values from -0.1875 to 0.1875
- gate_weight: bfloat16 [1024, 6, 256], P(None, None, 'tensor'), may hold values from -0.1875 to 0.1875
- beta_weight: bfloat16 [1024, 6], replicated, may hold values from -0.1875 to 0.1875
- decay_weight: bfloat16 [1024, 6], replicated, may hold values from -0.1875 to 0.1875
- q_conv: float32 [4, 768], replicated, may hold values from -3 to 3
- k_conv: float32 [4, 768], replicated, may hold values from -3 to 3
- v_conv: float32 [4, 6, 256], P(None, None, 'tensor'), may hold values from -3 to 3
- decay_scale: float32 [6], replicated, may hold values from 0.0009765625 to 0.05
- dt_bias: float32 [6], replicated, may hold values from -1 to 1
- out_gain: float32 [256], P('tensor'), may hold values from 0.5 to 1.5
- out_weight: bfloat16 [6, 256, 1024], P(None, 'tensor'), may hold values from -0.3125 to 0.3125
- norm2_gain: float32 [1024], replicated, may hold values from 0.5 to 1.5
- ffn_gate: bfloat16 [1024, 2816], P(None, 'tensor'), may hold values from -0.1875 to 0.1875
- ffn_up: bfloat16 [1024, 2816], P(None, 'tensor'), may hold values from -0.1875 to 0.1875
- ffn_down: bfloat16 [2816, 1024], P('tensor'), may hold values from -0.109375 to 0.109375
- cotangent: bfloat16 [1024, 1024], P(('dp', 'seq')), may hold values from -6 to 6
Outputs:
- block_output: bfloat16 [1024, 1024], P(('dp', 'seq'))
- grad_input: float32 [1024, 1024], P(('dp', 'seq'))
- grad_norm1_gain: float32 [1024], replicated
- grad_q_weight: float32 [1024, 768], replicated
- grad_k_weight: float32 [1024, 768], replicated
- grad_v_weight: float32 [1024, 6, 256], P(None, None, 'tensor')
- grad_gate_weight: float32 [1024, 6, 256], P(None, None, 'tensor')
- grad_beta_weight: float32 [1024, 6], replicated
- grad_decay_weight: float32 [1024, 6], replicated
- grad_q_conv: float32 [4, 768], replicated
- grad_k_conv: float32 [4, 768], replicated
- grad_v_conv: float32 [4, 6, 256], P(None, None, 'tensor')
- grad_decay_scale: float32 [6], replicated
- grad_dt_bias: float32 [6], replicated
- grad_out_gain: float32 [256], P('tensor')
- grad_out_weight: float32 [6, 256, 1024], P(None, 'tensor')
- grad_norm2_gain: float32 [1024], replicated
- grad_ffn_gate: float32 [1024, 2816], P(None, 'tensor')
- grad_ffn_up: float32 [1024, 2816], P(None, 'tensor')
- grad_ffn_down: float32 [2816, 1024], P('tensor')
All inputs are finite; a program needn't handle non-finite values.
Results may differ from a plain program's by a relative error of at most 0.025.
Values may be sent and summed in bfloat16 or wider, within the bound.
No kernel may reach another device: no remote copies, remote signals or barrier semaphores. Data moves between devices by JAX's collectives and lax.ppermute only.
A program may use at most 128 MiB of HBM per device.

v0:
```python
import jax
import jax.numpy as jnp
from jax import lax
from jax.sharding import PartitionSpec as P

DV = 256
SPAN = 64
EPS = 1e-06
HIGH_PRECISION = lax.Precision.HIGHEST


def from_behind(value, axis, by):
    length = lax.axis_size(axis)
    pairs = [(i, i + by) for i in range(length) if 0 <= i + by < length]
    return lax.ppermute(value, axis, pairs)


def matmul(left, right):
    return jnp.dot(left, right, preferred_element_type=jnp.float32)


def rms_scale(matrix, gain):
    return matrix * lax.rsqrt(jnp.mean(matrix * matrix, axis=-1, keepdims=True) + EPS) * gain


def swiglu(gate_act, up_act):
    return jax.nn.silu(gate_act) * up_act


def conv_silu(edge_rows, rows, conv_taps):
    length = rows.shape[0]
    padded = jnp.concatenate([edge_rows, rows], axis=0)
    summed = conv_taps[0] * padded[0:length]
    for offset in range(1, conv_taps.shape[0]):
        summed = summed + conv_taps[offset] * padded[offset : offset + length]
    return jax.nn.silu(summed)


def unit_rows(matrix):
    return matrix * lax.rsqrt(jnp.sum(matrix * matrix, axis=-1, keepdims=True) + EPS)


def mixer_inputs(
    q_proj,
    k_proj,
    v_proj,
    b_proj,
    a_proj,
    q_edge,
    k_edge,
    v_edge,
    q_conv,
    k_conv,
    v_conv,
    decay_scale,
    dt_bias,
):
    length = q_proj.shape[0]
    n_heads = b_proj.shape[1]
    queries = conv_silu(q_edge, q_proj, q_conv).reshape(length, n_heads, -1)
    key_vecs = conv_silu(k_edge, k_proj, k_conv).reshape(length, n_heads, -1)
    values = conv_silu(v_edge, v_proj, v_conv.reshape(v_conv.shape[0], -1)).reshape(
        length, n_heads, -1
    )
    queries = unit_rows(queries) * queries.shape[2] ** (-0.5)
    key_vecs = unit_rows(key_vecs)
    beta_gate = jax.nn.sigmoid(b_proj)
    log_decay = -decay_scale * jax.nn.softplus(a_proj + dt_bias)
    return (
        jnp.transpose(queries, (1, 0, 2)),
        jnp.transpose(key_vecs, (1, 0, 2)),
        jnp.transpose(values, (1, 0, 2)),
        beta_gate.T,
        log_decay.T,
    )


def gated_norm(head_out, gate_proj, gain, sum_squares):
    scale_rows = lax.rsqrt(sum_squares / DV + EPS)[..., None]
    return head_out * scale_rows * gain * jax.nn.silu(gate_proj)


def delta_run(queries, key_vecs, values, beta_gate, log_decay, start_state):
    n_heads, length, key_width = key_vecs.shape
    val_width = values.shape[2]
    n_blocks = length // SPAN
    q_blk = queries.reshape(n_heads, n_blocks, SPAN, key_width)
    k_blk = key_vecs.reshape(n_heads, n_blocks, SPAN, key_width)
    v_blk = values.reshape(n_heads, n_blocks, SPAN, val_width)
    b_blk = beta_gate.reshape(n_heads, n_blocks, SPAN)
    g_cum = jnp.cumsum(log_decay.reshape(n_heads, n_blocks, SPAN), axis=-1)
    places = jnp.arange(SPAN)
    strict = places[:, None] > places[None, :]
    within = places[:, None] >= places[None, :]
    differ = g_cum[..., :, None] - g_cum[..., None, :]
    decays = jnp.where(within, jnp.exp(jnp.where(within, differ, 0.0)), 0.0)
    k_gram = jnp.einsum("hnik,hnjk->hnij", k_blk, k_blk, precision=HIGH_PRECISION)
    l_mat = jnp.eye(SPAN, dtype=jnp.float32) + jnp.where(
        strict, b_blk[..., :, None] * k_gram * decays, 0.0
    )
    right_side = jnp.concatenate(
        [b_blk[..., None] * v_blk, (b_blk * jnp.exp(g_cum))[..., None] * k_blk], axis=-1
    )
    solved = lax.linalg.triangular_solve(
        l_mat, right_side, left_side=True, lower=True, unit_diagonal=True
    )
    updates = solved[..., :val_width]
    w_mat = solved[..., val_width:]
    qk_mat = jnp.einsum("hnik,hnjk->hnij", q_blk, k_blk, precision=HIGH_PRECISION) * decays
    g_last = g_cum[..., -1:]
    k_end = k_blk * jnp.exp(g_last - g_cum)[..., None]
    q_dec = q_blk * jnp.exp(g_cum)[..., None]

    def advance(current_state, block_in):
        (
            current_update_rows,
            current_write_rows,
            current_query_decayed,
            current_query_key,
            current_key_edge,
            current_gate_log,
        ) = block_in
        fresh_value_rows = current_update_rows - jnp.einsum(
            "nsz,nzu->nsu", current_write_rows, current_state, precision=HIGH_PRECISION
        )
        block_result = jnp.einsum(
            "nsz,nzu->nsu", current_query_decayed, current_state, precision=HIGH_PRECISION
        ) + jnp.einsum(
            "zdn,znb->zdb", current_query_key, fresh_value_rows, precision=HIGH_PRECISION
        )
        following_state = jnp.exp(current_gate_log)[..., None] * current_state + jnp.einsum(
            "ozq,ozp->oqp", current_key_edge, fresh_value_rows, precision=HIGH_PRECISION
        )
        return (following_state, block_result)

    blocks_in = tuple(
        (jnp.moveaxis(member, 1, 0) for member in (updates, w_mat, q_dec, qk_mat, k_end, g_last))
    )
    final_state, outputs = lax.scan(advance, start_state, blocks_in)
    return (jnp.moveaxis(outputs, 0, 1).reshape(n_heads, length, val_width), final_state)


def on_device(
    block_input,
    norm1_gain,
    q_weight,
    k_weight,
    v_weight,
    gate_weight,
    beta_weight,
    decay_weight,
    q_conv,
    k_conv,
    v_conv,
    decay_scale,
    dt_bias,
    out_gain,
    out_weight,
    norm2_gain,
    ffn_gate,
    ffn_up,
    ffn_down,
    cotangent,
):
    length = block_input.shape[0]
    model_width = block_input.shape[1]
    n_heads = beta_weight.shape[1]
    qk_cols = q_weight.shape[1]
    key_width = qk_cols // n_heads
    value_part = v_weight.shape[2]
    edge_count = q_conv.shape[0] - 1
    inputs_f = block_input.astype(jnp.float32)
    normed1, pull_norm1 = jax.vjp(rms_scale, inputs_f, norm1_gain)
    normed1_b = normed1.astype(jnp.bfloat16)
    v_mat = v_weight.reshape(model_width, -1)
    g_mat = gate_weight.reshape(model_width, -1)
    q_proj = matmul(normed1_b, q_weight)
    k_proj = matmul(normed1_b, k_weight)
    v_proj = matmul(normed1_b, v_mat)
    gate_proj = matmul(normed1_b, g_mat).reshape(length, n_heads, value_part)
    b_proj = matmul(normed1_b, beta_weight)
    a_proj = matmul(normed1_b, decay_weight)
    tail_rows = jnp.concatenate(
        [
            q_proj[length - edge_count :],
            k_proj[length - edge_count :],
            v_proj[length - edge_count :],
        ],
        axis=1,
    )
    edge_rows = from_behind(tail_rows, "seq", 1)
    prepared, pull_inputs = jax.vjp(
        mixer_inputs,
        q_proj,
        k_proj,
        v_proj,
        b_proj,
        a_proj,
        edge_rows[:, :qk_cols],
        edge_rows[:, qk_cols : 2 * qk_cols],
        edge_rows[:, 2 * qk_cols :],
        q_conv,
        k_conv,
        v_conv,
        decay_scale,
        dt_bias,
    )
    queries, key_vecs, values, beta_gate, log_decay = prepared
    empty_state = jnp.zeros((n_heads, key_width, value_part), jnp.float32)
    start_state = empty_state
    unused, end_state = delta_run(queries, key_vecs, values, beta_gate, log_decay, start_state)
    start_state = from_behind(end_state.astype(jnp.bfloat16), "seq", 1).astype(end_state.dtype)
    (mixed_heads, final_state), pull_delta = jax.vjp(
        delta_run, queries, key_vecs, values, beta_gate, log_decay, start_state
    )
    head_out = jnp.transpose(mixed_heads, (1, 0, 2))
    sum_squares = lax.psum(jnp.sum(head_out * head_out, axis=2), "tensor")
    gated, pull_gate = jax.vjp(gated_norm, head_out, gate_proj, out_gain, sum_squares)
    gated_b = gated.astype(jnp.bfloat16).reshape(length, -1)
    o_mat = out_weight.reshape(-1, model_width)
    mixer_total = lax.psum(matmul(gated_b, o_mat).astype(jnp.bfloat16), "tensor").astype(
        jnp.float32
    )
    hidden_res = inputs_f + mixer_total
    normed2, pull_norm2 = jax.vjp(rms_scale, hidden_res, norm2_gain)
    normed2_b = normed2.astype(jnp.bfloat16)
    inner, pull_ffn = jax.vjp(swiglu, matmul(normed2_b, ffn_gate), matmul(normed2_b, ffn_up))
    inner_b = inner.astype(jnp.bfloat16)
    ffn_total = lax.psum(matmul(inner_b, ffn_down).astype(jnp.bfloat16), "tensor").astype(
        jnp.float32
    )
    block_output = (hidden_res + ffn_total).astype(jnp.bfloat16)
    grad_inner = matmul(cotangent, ffn_down.T)
    grad_down = matmul(inner_b.T, cotangent)
    grad_gate_act, grad_up_act = pull_ffn(grad_inner)
    gate_grad_b = grad_gate_act.astype(jnp.bfloat16)
    up_grad_b = grad_up_act.astype(jnp.bfloat16)
    grad_ffn_gate = matmul(normed2_b.T, gate_grad_b)
    grad_ffn_up = matmul(normed2_b.T, up_grad_b)
    normed2_part = matmul(gate_grad_b, ffn_gate.T) + matmul(up_grad_b, ffn_up.T)
    grad_normed2 = lax.psum(normed2_part.astype(jnp.bfloat16), "tensor").astype(jnp.float32)
    grad_hidden_n, grad_norm2 = pull_norm2(grad_normed2)
    grad_hidden = cotangent.astype(jnp.float32) + grad_hidden_n
    grad_hidden_b = grad_hidden.astype(jnp.bfloat16)
    grad_gated = matmul(grad_hidden_b, o_mat.T).reshape(length, n_heads, value_part)
    grad_out_weight = matmul(gated_b.T, grad_hidden_b).reshape(out_weight.shape)
    heads_local, grad_gate_proj, grad_out_gain, squares_local = pull_gate(grad_gated)
    grad_squares = lax.psum(squares_local, "tensor")
    grad_heads = heads_local + 2.0 * head_out * grad_squares[..., None]
    grad_mixed = jnp.transpose(grad_heads, (1, 0, 2))
    end_grad = empty_state
    hop_terms = pull_delta((grad_mixed, end_grad))
    end_grad = from_behind(hop_terms[5].astype(jnp.bfloat16), "seq", -1).astype(jnp.float32)
    full_terms = pull_delta((grad_mixed, end_grad))
    delta_grads = tuple((full_terms[member] for member in range(5)))
    input_grads = pull_inputs(delta_grads)
    edge_grads = jnp.concatenate([input_grads[5], input_grads[6], input_grads[7]], axis=1)
    edge_back = from_behind(edge_grads, "seq", -1)
    q_grad_rows = input_grads[0].at[length - edge_count :].add(edge_back[:, :qk_cols])
    k_grad_rows = input_grads[1].at[length - edge_count :].add(edge_back[:, qk_cols : 2 * qk_cols])
    v_grad_rows = input_grads[2].at[length - edge_count :].add(edge_back[:, 2 * qk_cols :])
    qg_b = q_grad_rows.astype(jnp.bfloat16)
    kg_b = k_grad_rows.astype(jnp.bfloat16)
    vg_b = v_grad_rows.astype(jnp.bfloat16)
    bg_b = input_grads[3].astype(jnp.bfloat16)
    ag_b = input_grads[4].astype(jnp.bfloat16)
    gg_b = grad_gate_proj.reshape(length, -1).astype(jnp.bfloat16)
    normed1_part = (
        matmul(qg_b, q_weight.T)
        + matmul(kg_b, k_weight.T)
        + matmul(vg_b, v_mat.T)
        + matmul(gg_b, g_mat.T)
        + matmul(bg_b, beta_weight.T)
        + matmul(ag_b, decay_weight.T)
    )
    grad_input_n, grad_norm1 = pull_norm1(normed1_part)
    grad_input = grad_hidden + lax.psum(grad_input_n.astype(jnp.bfloat16), "tensor").astype(
        jnp.float32
    )
    shared = lax.psum(
        (
            grad_norm1,
            matmul(normed1_b.T, qg_b),
            matmul(normed1_b.T, kg_b),
            matmul(normed1_b.T, bg_b),
            matmul(normed1_b.T, ag_b),
            input_grads[8],
            input_grads[9],
            input_grads[11],
            input_grads[12],
        ),
        ("dp", "seq", "tensor"),
    )
    value_grad = matmul(normed1_b.T, vg_b).reshape(v_weight.shape)
    gate_grad = matmul(normed1_b.T, gg_b).reshape(gate_weight.shape)
    split = (
        lax.psum(value_grad.astype(jnp.bfloat16), ("dp", "seq")).astype(jnp.float32),
        lax.psum(gate_grad.astype(jnp.bfloat16), ("dp", "seq")).astype(jnp.float32),
        lax.psum(input_grads[10].astype(jnp.bfloat16), ("dp", "seq")).astype(jnp.float32),
        lax.psum(grad_out_gain.astype(jnp.bfloat16), ("dp", "seq")).astype(jnp.float32),
        lax.psum(grad_out_weight.astype(jnp.bfloat16), ("dp", "seq")).astype(jnp.float32),
        lax.psum(grad_norm2.astype(jnp.bfloat16), ("dp", "seq")).astype(jnp.float32),
        lax.psum(grad_ffn_gate.astype(jnp.bfloat16), ("dp", "seq")).astype(jnp.float32),
        lax.psum(grad_ffn_up.astype(jnp.bfloat16), ("dp", "seq")).astype(jnp.float32),
        lax.psum(grad_down.astype(jnp.bfloat16), ("dp", "seq")).astype(jnp.float32),
    )
    return (
        block_output,
        grad_input,
        shared[0],
        shared[1],
        shared[2],
        split[0],
        split[1],
        shared[3],
        shared[4],
        shared[5],
        shared[6],
        split[2],
        shared[7],
        shared[8],
        split[3],
        split[4],
        split[5],
        split[6],
        split[7],
        split[8],
    )


def solution(mesh):
    placed = (
        P(("dp", "seq"), None),
        P(),
        P(),
        P(),
        P(None, None, "tensor"),
        P(None, None, "tensor"),
        P(),
        P(),
        P(),
        P(),
        P(None, None, "tensor"),
        P(),
        P(),
        P("tensor"),
        P(None, "tensor", None),
        P(),
        P(None, "tensor"),
        P(None, "tensor"),
        P("tensor", None),
        P(("dp", "seq"), None),
    )
    return jax.shard_map(
        on_device,
        mesh=mesh,
        in_specs=placed,
        out_specs=(
            P(("dp", "seq"), None),
            P(("dp", "seq"), None),
            P(),
            P(),
            P(),
            P(None, None, "tensor"),
            P(None, None, "tensor"),
            P(),
            P(),
            P(),
            P(),
            P(None, None, "tensor"),
            P(),
            P(),
            P("tensor"),
            P(None, "tensor", None),
            P(),
            P(None, "tensor"),
            P(None, "tensor"),
            P("tensor", None),
        ),
        check_vma=False,
    )
```

profile of v0, /device:TPU:0, one launch (start us, length us, event | category | flops | bytes accessed | tf_op | source)
XLA Modules:
  0.0 872.2 jit_solution(6370596105471412092)
XLA Ops:
  13.4 2.4 collective-permute-start
  27.3 59.7 %custom-call.11 = f32[6,2,1,64,64]{3,4,2,1,0:T(8,128)S(1)} custom-call(f32[6,2,1,64,64]{4,3,2,1,0:T(8,128)} %get-tuple-element.1082), custom_call_target="InvertDiagBlocksLowerTriangular" | custom-call | tf_op jit(solution)/shard_map/triangular_solve/custom-call.1 | solution.py:104
  88.1 2.0 fusion.103
  91.2 2.0 while.77
  93.8 1.9 collective-permute-start.1
  95.8 2.7 fusion.145
  101.2 1.9 copy.179
  103.2 2.7 bitcast_multiply_fusion.11
  109.3 9.7 %while.75 = (s32[]{:T(128)}, f32[6,128,64]{1,2,0:T(8,128)S(1)}, f32[2,6,64,64]{3,2,1,0:T(8,128)}, f32[2,6,128,64]{2,3,1,0:T(8,128)}, f32[2,6,64,64]{3,2,1,0:T(8,...) while((s32[]{:T(128)}, f32[6,128,64]{1,2,0:T(8,128)S(1)}, ...), condition=%wide.region_7.9_spmd, body=%wide.region_6.8_spmd.sunk | while | flops 132268032 | bytes 5707657 | solution.py:139
  119.6 1.9 copy.188
  122.8 10.7 %psum.168 = f32[128,6]{0,1:T(8,128)S(1)} all-reduce(f32[128,6]{0,1:T(8,128)S(1)} %fusion.174), channel_id=1, replica_groups=mesh['dp'=4,'seq'=2,'tensor'=4] {'tensor'}, use_global_device_ids=true, to_apply=%region_9.11 | all-reduce | flops 768 | bytes 6144 | tf_op jit(solution)/shard_map/psum | solution.py:217
  134.7 2.2 multiply_convert_fusion.3
  138.5 1.9 copy.193
  140.4 40.1 %all-reduce.39.cloned.1.call-done = bf16[128,1024]{1,0:T(8,128)(2,1)} async-done(((bf16[128,1024]{1,0:T(8,128)(2,1)}), bf16[128,1024]{1,0:T(8,128)(2,1)}) %all-reduce.39.cloned.1.call-update) | async-done | bytes 262160 | tf_op jit(solution)/shard_map/psum | solution.py:221
  182.9 2.0 fusion.242
  192.8 2.7 convolution_convert_fusion.2
  195.5 40.5 %all-reduce.41.cloned.1.call-done = bf16[128,1024]{1,0:T(8,128)(2,1)} async-done(((bf16[128,1024]{1,0:T(8,128)(2,1)}), bf16[128,1024]{1,0:T(8,128)(2,1)}) %all-reduce.41.cloned.1.call-update) | async-done | bytes 262160 | tf_op jit(solution)/shard_map/psum | solution.py:241
  236.0 1.9 fusion.120
  242.3 8.9 %psum.172 = f32[128,6]{0,1:T(8,128)S(1)} all-reduce(f32[128,6]{0,1:T(8,128)S(1)} %get-tuple-element.1089), channel_id=1, replica_groups=mesh['dp'=4,'seq'=2,'tensor'=4] {'tensor'}, use_global_device_ids=true, to_apply=%region_16.18 | all-reduce | flops 768 | bytes 6144 | tf_op jit(solution)/shard_map/psum | solution.py:248
  254.3 8.5 while.78
  264.2 2.3 convolution_bitcast_fusion.4
  270.4 20.2 %while.76 = (s32[]{:T(128)}, f32[6,128,64]{1,2,0:T(8,128)S(1)}, f32[2,6,64,64]{3,2,1,0:T(8,128)}, f32[2,6,64,128]{3,2,1,0:T(8,128)}, f32[2,6,64,128]{3,2,0,1:T(8...) while((s32[]{:T(128)}, f32[6,128,64]{1,2,0:T(8,128)S(1)}, ...), condition=%wide.region_21.23_spmd, body=%wide.region_19.22_spmd.sunk | while | flops 264560640 | bytes 16820268 | solution.py:139
  271.6 2.0 fusion.394
  281.6 1.9 fusion.394
  291.2 2.3 fusion.111
  295.9 2.4 multiply_reduce_fusion.10
  304.3 2.0 copy.214
  310.0 1.8 add_add_fusion.3
  313.0 2.6 multiply_reduce_fusion.3
  321.8 2.1 multiply_reduce_fusion.17
  327.5 1.8 fusion.229
  336.9 4.0 reduce_window_sum.25
  341.0 2.1 fusion.231
  350.6 2.4 fusion.247
  354.3 2.6 convolution_add_fusion.13
  359.1 1.8 fusion.94
  371.1 2.3 fusion.248
  373.4 2.3 fusion.246
  376.5 30.4 %all-reduce.29 = (bf16[4,6,64]{2,1,0:T(8,128)(2,1)S(1)}, bf16[64]{0:T(256)(128)(2,1)S(1)}, bf16[1024]{0:T(1024)(128)(2,1)S(1)}) all-reduce(bf16[4,6,64]{2,1,0:T(8,128)(2,1)S(1)} %convert_element_type.192, bf16[64]{0:T(256)(128)(2,1)S(1)} %copy-done.180, ...), channel_id=1, replica_groups=mesh['dp'=4,'seq'=2,'tensor'=4] {'dp','seq'}, use_global_device_ids=true, to_apply=%region_57.59 | all-reduce | flops 2624 | bytes 10496 | tf_op jit(solution)/shard_map/psum | solution.py:299
  411.8 1.8 convert_add_fusion.1
  413.6 144.4 %all-reduce.47.cloned.1.call-done = (bf16[1024,6,64]{0,2,1:T(8,128)(2,1)}, bf16[1024,6,64]{0,2,1:T(8,128)(2,1)}, bf16[6,64,1024]{2,1,0:T(8,128)(2,1)}, bf16[1024...) async-done(((bf16[1024,6,64]{0,2,1:T(8,128)(2,1)}, bf16[1024,6,64]{0,2,1:T(8,128)(2,1)}, bf16[6,64,1024]{2,1,0:T(8,128)(2,1)}, ...) | async-done | bytes 6684688 | tf_op jit(solution)/shard_map/psum | solution.py:297
  558.1 2.5 convert_element_type.187
  563.8 1.9 convert_element_type.201
  565.8 1.9 convert_element_type.203
  567.7 1.9 convert_element_type.205
  569.7 121.7 %all-reduce.43.cloned.1.call-done = (f32[1024]{0:T(1024)}, f32[1024,6]{0,1:T(8,128)}, f32[1024,6]{0,1:T(8,128)}, f32[4,768]{1,0:T(4,128)}, f32[4,768]{1,0:T(4,128)}, /*index=5*/f32[6]{0:T(128)}, f32[6]{0:T(128)}) async-done(((f32[1024]{0:T(1024)}, f32[1024,6]{0,1:T(8,128)}, f32[1024,6]{0,1:T(8,128)}, f32[4,768]{1,0:T(4,128)}, f32[4,768]{1,0:T(4,128)}, /*index=5*/f32[6]{0:T(128)}, f32[6]{0:T(128)}), ...) | async-done | bytes 77888 | tf_op jit(solution)/shard_map/psum | solution.py:280
  691.4 163.4 %all-reduce.45.cloned.1.call-done = (f32[1024,768]{1,0:T(8,128)}, f32[1024,768]{1,0:T(8,128)}) async-done(((f32[1024,768]{1,0:T(8,128)}, f32[1024,768]{1,0:T(8,128)}), (f32[1024,768]{1,0:T(8,128)}, f32[1024,768]{1,0:T(8,128)})) %all-reduce.45.cloned.1.call-update) | async-done | bytes 6291472 | tf_op jit(solution)/shard_map/psum | solution.py:280
  856.1 3.9 copy.411
  (661 shorter events, 156.0 us)
Async XLA Ops:
  7.2 173.3 %all-reduce.39.cloned.1.call-start = ((), (), s32[]{:S(2)}) async-start(), calls=%async_computation | async-start | bytes 524288 | tf_op jit(solution)/shard_map/psum | solution.py:221
  10.6 7.7 copy-start.1
  11.0 10.9 %copy-start.39 = (f32[128,768]{1,0:T(8,128)}, f32[128,768]{1,0:T(8,128)S(1)}, u32[]{:S(2)}) copy-start(f32[128,768]{1,0:T(8,128)S(1)} %fusion.239) | copy-start | bytes 1179652
  11.5 13.4 %copy-start.70 = (f32[128,384]{1,0:T(8,128)}, f32[128,384]{1,0:T(8,128)S(1)}, u32[]{:S(2)}) copy-start(f32[128,384]{1,0:T(8,128)S(1)} %fusion.240) | copy-start | bytes 589828
  11.5 6.8 copy-start.104
  11.5 7.3 copy-start.159
  11.5 7.4 copy-start.160
  12.3 6.7 copy-start.161
  13.4 7.9 collective-permute-start
  18.5 5.4 copy-start.130
  18.6 7.5 copy-start.91
  18.8 5.1 copy-start.120
  18.8 5.1 copy-start.122
  18.8 5.1 copy-start.124
  18.9 5.1 copy-start.126
  19.0 7.2 copy-start.100
  20.3 5.8 copy-start.102
  26.1 61.9 %copy-start.45 = (f32[6,128,64]{2,1,0:T(8,128)}, f32[6,128,64]{2,1,0:T(8,128)S(1)}, u32[]{:S(2)}) copy-start(f32[6,128,64]{2,1,0:T(8,128)S(1)} %copy.172) | copy-start | bytes 589828
  93.8 13.0 %collective-permute-start.1 = (bf16[6,128,64]{1,2,0:T(8,128)(2,1)}, bf16[6,128,64]{1,2,0:T(8,128)(2,1)}, u32[]{:S(2)}, u32[]{:S(2)}) collective-permute-start(bf16[6,128,64]{1,2,0:T(8,128)(2,1)} %convert_element_type.159), channel_id=1, source_target_pairs={{0,4},{1,5},{2,6},{3,7},{8,12},{9,13},{10,14},{11,15},{16,20},{17,... | collective-permute-start | bytes 294920 | tf_op jit(solution)/shard_map/ppermute | solution.py:15
  99.7 6.2 copy-start.10
  119.0 15.7 %copy-start.2 = (bf16[128,1024]{1,0:T(8,128)(2,1)S(1)}, bf16[128,1024]{1,0:T(8,128)(2,1)}, u32[]{:S(2)}) copy-start(bf16[128,1024]{1,0:T(8,128)(2,1)} %copy-done.1) | copy-start | bytes 786436
  119.0 15.7 %copy-start.181 = (f32[64]{0:T(128)S(1)}, f32[64]{0:T(128)}, u32[]{:S(2)}) copy-start(f32[64]{0:T(128)} %param.49) | copy-start | bytes 772
  136.9 46.0 %copy-start.87 = (bf16[128,6,64]{0,2,1:T(8,128)(2,1)}, bf16[128,6,64]{0,2,1:T(8,128)(2,1)S(1)}, u32[]{:S(2)}) copy-start(bf16[128,6,64]{0,2,1:T(8,128)(2,1)S(1)} %get-tuple-element.1094) | copy-start | bytes 294916
  136.9 43.6 %copy-start.4 = (bf16[128,1024]{1,0:T(8,128)(2,1)S(1)}, bf16[128,1024]{1,0:T(8,128)(2,1)}, u32[]{:S(2)}) copy-start(bf16[128,1024]{1,0:T(8,128)(2,1)} %param.36) | copy-start | bytes 786436
  136.9 44.9 %copy-start.110 = (f32[1024]{0:T(1024)S(1)}, f32[1024]{0:T(1024)}, u32[]{:S(2)}) copy-start(f32[1024]{0:T(1024)} %param.51) | copy-start | bytes 12292
  138.0 98.0 %all-reduce.41.cloned.1.call-start = ((), (), s32[]{:S(2)}) async-start(), calls=%async_computation.1 | async-start | bytes 524288 | tf_op jit(solution)/shard_map/psum | solution.py:241
  192.7 217.3 %all-reduce.49.cloned.1.call-start = ((), (), s32[]{:S(2)}) async-start(), calls=%async_computation.5 | async-start | bytes 1048576 | tf_op jit(solution)/shard_map/psum | solution.py:229
  239.3 12.0 %copy-start.95 = (f32[128,6,64]{0,2,1:T(8,128)S(1)}, f32[128,6,64]{0,2,1:T(8,128)}, u32[]{:S(2)}) copy-start(f32[128,6,64]{0,2,1:T(8,128)} %get-tuple-element.1095) | copy-start | bytes 589828
  254.3 9.9 %copy-start.89 = (bf16[128,6,64]{0,2,1:T(8,128)(2,1)S(1)}, bf16[128,6,64]{0,2,1:T(8,128)(2,1)}, u32[]{:S(2)}) copy-start(bf16[128,6,64]{0,2,1:T(8,128)(2,1)} %get-tuple-element.1055) | copy-start | bytes 294916
  262.9 3.6 collective-permute-start.2
  270.4 4.9 copy-start.6
  270.5 4.9 copy-start.54
  280.5 4.9 copy-start.6
  280.5 4.9 copy-start.54
  321.8 7.4 copy-start.97
  321.8 7.4 copy-start.108
  321.8 11.6 %copy-start.93 = (f32[6,2,64]{2,1,0:T(2,128)S(1)}, f32[6,2,64]{2,1,0:T(2,128)}, u32[]{:S(2)}) copy-start(f32[6,2,64]{2,1,0:T(2,128)} %copy-done.91) | copy-start | bytes 9220
  324.7 23.6 %copy-start.19 = (f32[128,768]{1,0:T(8,128)S(1)}, f32[128,768]{1,0:T(8,128)}, u32[]{:S(2)}) copy-start(f32[128,768]{1,0:T(8,128)} %copy-done.18) | copy-start | bytes 1179652
  324.7 23.6 %copy-start.21 = (f32[128,768]{1,0:T(8,128)S(1)}, f32[128,768]{1,0:T(8,128)}, u32[]{:S(2)}) copy-start(f32[128,768]{1,0:T(8,128)} %copy-done.20) | copy-start | bytes 1179652
  326.2 22.2 %collective-permute-start.3 = (f32[3,1920]{1,0:T(4,128)}, f32[3,1920]{1,0:T(4,128)}, u32[]{:S(2)}, u32[]{:S(2)}) collective-permute-start(f32[3,1920]{1,0:T(4,128)} %pad_maximum_fusion.4), channel_id=1, source_target_pairs={{4,0},{5,1},{6,2},{7,3},{12,8},{13,9},{14,10},{15,11},{20,16},{21,... | collective-permute-start | bytes 69128 | tf_op jit(solution)/shard_map/ppermute | solution.py:15
  341.0 7.4 copy-start.23
  341.0 7.4 copy-start.25
  341.0 7.4 copy-start.27
  349.1 5.2 copy-start.29
  363.1 194.9 %all-reduce.47.cloned.1.call-start = ((), (), s32[]{:S(2)}) async-start(), calls=%async_computation.4 | async-start | bytes 13369344 | tf_op jit(solution)/shard_map/psum | solution.py:297
  367.1 324.3 %all-reduce.43.cloned.1.call-start = ((), (), s32[]{:S(2)}) async-start(), calls=%async_computation.2 | async-start | bytes 190464 | tf_op jit(solution)/shard_map/psum | solution.py:280
  373.4 481.5 %all-reduce.45.cloned.1.call-start = ((), (), s32[]{:S(2)}) async-start(), calls=%async_computation.3 | async-start | bytes 12582912 | tf_op jit(solution)/shard_map/psum | solution.py:280
  375.7 34.3 %copy-start.17 = (bf16[128,1024]{1,0:T(8,128)(2,1)S(1)}, bf16[128,1024]{1,0:T(8,128)(2,1)}, u32[]{:S(2)}) copy-start(bf16[128,1024]{1,0:T(8,128)(2,1)} %all-reduce.39.cloned.1.call-done) | copy-start | bytes 786436
  (168 other events, 410.7 us)
Sparse Core Ops, SparseCore 0:
  138.1 42.4 all-reduce.38
  192.9 43.0 all-reduce.40
  363.2 46.7 all-reduce.48
  414.5 143.5 all-reduce.46
  565.5 125.8 all-reduce.42
  697.6 157.1 all-reduce.44
where the time goes:
time: 883 us; the launch traced here: 872 us
  waiting for transfers between devices  512 us (58%)
  other arithmetic  132 us (15%)
  matrix products  86.7 us (10%)
  local copies, waits for them, and re-layouts  66.9 us (8%)
  blocking collectives  50.1 us (6%)
  between operations  16.5 us (2%)
    psum x2, waiting for transfers between devices, on_device(): lax.psum((grad_norm1, matmul(normed1_b.T, qg_b), matmul(normed1_b.T, kg_b...  285 us
    psum x1, waiting for transfers between devices, on_device(): lax.psum(value_grad.astype(jnp.bfloat16), ('dp', 'seq')).astype(jnp.float32)  144 us
    another operation x5, other arithmetic, delta_run(): lax.linalg.triangular_solve(l_mat, right_side, left_side=True, lower=True...  61 us
    psum x1, waiting for transfers between devices, on_device(): lax.psum(normed2_part.astype(jnp.bfloat16), 'tensor').astype(jnp.float32)  40.5 us
    psum x1, waiting for transfers between devices, on_device(): lax.psum(matmul(gated_b, o_mat).astype(jnp.bfloat16), 'tensor')  40.1 us
    dot_general x30, matrix products, matmul(): return jnp.dot(left, right, preferred_element_type=jnp.float32)  38.7 us
    psum x1, blocking collectives, on_device(): lax.psum(input_grads[10].astype(jnp.bfloat16), ('dp', 'seq'))  30.4 us
    unnamed x363, local copies, waits for them, and re-layouts  25.5 us
  transfers between devices with their start and end apart: 10, of which 6 were waited for; matrix products, arithmetic and copies ran while one was open for 8% of the time, Pallas kernels for 0%

commit v1 on v0

--- a/solution.py
+++ b/solution.py
@@ -277,20 +277,19 @@
     grad_input = grad_hidden + lax.psum(grad_input_n.astype(jnp.bfloat16), "tensor").astype(
         jnp.float32
     )
-    shared = lax.psum(
-        (
-            grad_norm1,
-            matmul(normed1_b.T, qg_b),
-            matmul(normed1_b.T, kg_b),
-            matmul(normed1_b.T, bg_b),
-            matmul(normed1_b.T, ag_b),
-            input_grads[8],
-            input_grads[9],
-            input_grads[11],
-            input_grads[12],
-        ),
-        ("dp", "seq", "tensor"),
-    )
+    shared = (
+        grad_norm1,
+        matmul(normed1_b.T, qg_b),
+        matmul(normed1_b.T, kg_b),
+        matmul(normed1_b.T, bg_b),
+        matmul(normed1_b.T, ag_b),
+        input_grads[8],
+        input_grads[9],
+        input_grads[11],
+        input_grads[12],
+    )
+    for over in (("seq", "tensor"), "dp"):
+        shared = lax.psum(shared, over)
     value_grad = matmul(normed1_b.T, vg_b).reshape(v_weight.shape)
     gate_grad = matmul(normed1_b.T, gg_b).reshape(gate_weight.shape)
     split = (

time: 883 us -> 1020 us (1.16)
  waiting for transfers between devices: 512 us -> 647 us
    psum x2 -> x4, waiting for transfers between devices: 285 us -> 401 us  [on_device(): shared = lax.psum(shared, over)]
    psum x1, waiting for transfers between devices: 1.43 us -> 18.1 us  [on_device(): lax.psum(matmul(inner_b, ffn_down).astype(jnp.bfloat16), 'tensor')]
    unnamed x363 -> x383, local copies, waits for them, and re-layouts: 25.5 us -> 25.3 us
  transfers between devices with their start and end apart: 10 -> 12, of which waited for: 6 -> 8; matrix products, arithmetic and copies ran while one was open for 8% -> 7% of each run, Pallas kernels for 0% -> 0%
where the time goes in v1:
time: 1020 us; the launch traced here: 1010 us
  waiting for transfers between devices  647 us (63%)
  other arithmetic  129 us (13%)
  matrix products  86.2 us (8%)
  local copies, waits for them, and re-layouts  73.1 us (7%)
  blocking collectives  48 us (5%)
  between operations  16.6 us (2%)
    psum x4, waiting for transfers between devices, on_device(): shared = lax.psum(shared, over)  401 us
    psum x1, waiting for transfers between devices, on_device(): lax.psum(value_grad.astype(jnp.bfloat16), ('dp', 'seq')).astype(jnp.float32)  144 us
    another operation x5, other arithmetic, delta_run(): lax.linalg.triangular_solve(l_mat, right_side, left_side=True, lower=True...  61 us
    psum x1, waiting for transfers between devices, on_device(): lax.psum(matmul(gated_b, o_mat).astype(jnp.bfloat16), 'tensor')  42 us
    psum x1, waiting for transfers between devices, on_device(): lax.psum(normed2_part.astype(jnp.bfloat16), 'tensor').astype(jnp.float32)  41.2 us
    dot_general x30, matrix products, matmul(): return jnp.dot(left, right, preferred_element_type=jnp.float32)  37.4 us
    psum x1, blocking collectives, on_device(): lax.psum(input_grads[10].astype(jnp.bfloat16), ('dp', 'seq'))  28.3 us
    unnamed x383, local copies, waits for them, and re-layouts  25.3 us
  transfers between devices with their start and end apart: 12, of which 8 were waited for; matrix products, arithmetic and copies ran while one was open for 7% of the time, Pallas kernels for 0%

profile of v1, /device:TPU:0, one launch (start us, length us, event | category | flops | bytes accessed | tf_op | source)
XLA Modules:
  0.0 1008.5 jit_solution(4679060872180510569)
XLA Ops:
  13.4 2.4 collective-permute-start
  27.4 59.7 %custom-call.11 = f32[6,2,1,64,64]{3,4,2,1,0:T(8,128)S(1)} custom-call(f32[6,2,1,64,64]{4,3,2,1,0:T(8,128)} %get-tuple-element.1091), custom_call_target="InvertDiagBlocksLowerTriangular" | custom-call | tf_op jit(solution)/shard_map/triangular_solve/custom-call.1 | solution.py:104
  88.1 2.1 fusion.103
  91.2 2.0 while.77
  93.9 1.9 collective-permute-start.1
  95.8 2.8 fusion.145
  101.3 1.9 copy.179
  103.2 2.7 bitcast_multiply_fusion.11
  109.3 9.7 while.75
  119.6 1.9 copy.188
  122.8 10.7 %psum.231 = f32[128,6]{0,1:T(8,128)S(1)} all-reduce(f32[128,6]{0,1:T(8,128)S(1)} %fusion.174), channel_id=1, replica_groups=mesh['dp'=4,'seq'=2,'tensor'=4] {'tensor'}, use_global_device_ids=true, to_apply=%region_9.11 | all-reduce | flops 768 | bytes 6144 | tf_op jit(solution)/shard_map/psum | solution.py:217
  134.2 2.3 multiply_convert_fusion.3
  138.6 42.0 %all-reduce.43.cloned.1.call-done = bf16[128,1024]{1,0:T(8,128)(2,1)} async-done(((bf16[128,1024]{1,0:T(8,128)(2,1)}), bf16[128,1024]{1,0:T(8,128)(2,1)}) %all-reduce.43.cloned.1.call-update) | async-done | bytes 262160 | tf_op jit(solution)/shard_map/psum | solution.py:221
  183.0 2.0 fusion.242
  188.8 1.9 copy.193
  190.8 41.2 %all-reduce.45.cloned.1.call-done = bf16[128,1024]{1,0:T(8,128)(2,1)} async-done(((bf16[128,1024]{1,0:T(8,128)(2,1)}), bf16[128,1024]{1,0:T(8,128)(2,1)}) %all-reduce.45.cloned.1.call-update) | async-done | bytes 262160 | tf_op jit(solution)/shard_map/psum | solution.py:241
  231.9 1.9 fusion.120
  236.7 2.4 multiply_reduce_fusion.14
  239.7 8.9 psum.235
  251.7 8.5 while.78
  261.5 2.3 convolution_bitcast_fusion.4
  267.8 20.2 %while.76 = (s32[]{:T(128)}, f32[6,128,64]{1,2,0:T(8,128)S(1)}, f32[2,6,64,64]{3,2,1,0:T(8,128)}, f32[2,6,64,128]{3,2,1,0:T(8,128)}, f32[2,6,64,128]{3,2,0,1:T(8...) while((s32[]{:T(128)}, f32[6,128,64]{1,2,0:T(8,128)S(1)}, ...), condition=%wide.region_21.23_spmd, body=%wide.region_19.22_spmd.sunk | while | flops 264560640 | bytes 16820268 | solution.py:139
  269.0 1.9 fusion.394
  279.0 1.9 fusion.394
  288.6 2.3 fusion.111
  293.3 2.5 multiply_reduce_fusion.10
  298.3 1.9 copy.213
  303.1 2.0 copy.214
  305.1 2.4 convolution_add_fusion.17
  307.5 1.9 copy.202
  313.6 3.3 multiply_reduce_fusion.3
  324.0 1.9 multiply_reduce_fusion.17
  337.3 4.0 reduce_window_sum.25
  357.0 2.4 fusion.247
  359.5 2.3 fusion.248
  366.9 2.3 fusion.246
  381.0 41.4 %all-reduce.47.cloned.1.call-done = (f32[1024]{0:T(1024)}, f32[1024,6]{0,1:T(8,128)}, f32[1024,6]{0,1:T(8,128)}, f32[4,768]{1,0:T(4,128)}, f32[4,768]{1,0:T(4,128)}, /*index=5*/f32[6]{0:T(128)}, f32[6]{0:T(128)}) async-done(((f32[1024]{0:T(1024)}, f32[1024,6]{0,1:T(8,128)}, f32[1024,6]{0,1:T(8,128)}, f32[4,768]{1,0:T(4,128)}, f32[4,768]{1,0:T(4,128)}, /*index=5*/f32[6]{0:T(128)}, f32[6]{0:T(128)}), ...) | async-done | bytes 77888 | tf_op jit(solution)/shard_map/psum | solution.py:292
  422.5 108.2 %all-reduce.49.cloned.1.call-done = (f32[1024,768]{1,0:T(8,128)}, f32[1024,768]{1,0:T(8,128)}) async-done(((f32[1024,768]{1,0:T(8,128)}, f32[1024,768]{1,0:T(8,128)}), (f32[1024,768]{1,0:T(8,128)}, f32[1024,768]{1,0:T(8,128)})) %all-reduce.49.cloned.1.call-update) | async-done | bytes 6291472 | tf_op jit(solution)/shard_map/psum | solution.py:292
  531.5 28.3 %all-reduce.31 = (bf16[4,6,64]{2,1,0:T(8,128)(2,1)S(1)}, bf16[64]{0:T(256)(128)(2,1)S(1)}, bf16[1024]{0:T(1024)(128)(2,1)S(1)}) all-reduce(bf16[4,6,64]{2,1,0:T(8,128)(2,1)S(1)} %convert_element_type.192, bf16[64]{0:T(256)(128)(2,1)S(1)} %copy-done.191, ...), channel_id=1, replica_groups=mesh['dp'=4,'seq'=2,'tensor'=4] {'dp','seq'}, use_global_device_ids=true, to_apply=%region_64.66 | all-reduce | flops 2624 | bytes 10496 | tf_op jit(solution)/shard_map/psum | solution.py:298
  561.5 18.1 %all-reduce.57.cloned.1.call-done = (bf16[128,1024]{1,0:T(8,128)(2,1)}, bf16[128,1024]{1,0:T(8,128)(2,1)}) async-done(((bf16[128,1024]{1,0:T(8,128)(2,1)}, bf16[128,1024]{1,0:T(8,128)(2,1)}), (bf16[128,1024]{1,0:T(8,128)(2,1)}, bf16[128,1024]{1,0:T(8,128)(2,1)})) %all-reduce.57.cloned.1.call-update) | async-done | bytes 524304 | tf_op jit(solution)/shard_map/psum | solution.py:229
  583.2 144.4 %all-reduce.55.cloned.1.call-done = (bf16[1024,6,64]{0,2,1:T(8,128)(2,1)}, bf16[1024,6,64]{0,2,1:T(8,128)(2,1)}, bf16[6,64,1024]{2,1,0:T(8,128)(2,1)}, bf16[1024...) async-done(((bf16[1024,6,64]{0,2,1:T(8,128)(2,1)}, bf16[1024,6,64]{0,2,1:T(8,128)(2,1)}, bf16[6,64,1024]{2,1,0:T(8,128)(2,1)}, ...) | async-done | bytes 6684688 | tf_op jit(solution)/shard_map/psum | solution.py:296
  727.6 2.5 convert_element_type.187
  733.4 1.9 convert_element_type.201
  735.4 1.9 convert_element_type.203
  737.3 1.9 convert_element_type.205
  739.2 26.7 %all-reduce.51.cloned.1.call-done = (f32[1024]{0:T(1024)}, f32[1024,6]{0,1:T(8,128)}, f32[1024,6]{0,1:T(8,128)}, f32[4,768]{1,0:T(4,128)}, f32[4,768]{1,0:T(4,128)}, /*index=5*/f32[6]{0:T(128)}, f32[6]{0:T(128)}) async-done(((f32[1024]{0:T(1024)}, f32[1024,6]{0,1:T(8,128)}, f32[1024,6]{0,1:T(8,128)}, f32[4,768]{1,0:T(4,128)}, f32[4,768]{1,0:T(4,128)}, /*index=5*/f32[6]{0:T(128)}, f32[6]{0:T(128)}), ...) | async-done | bytes 77888 | tf_op jit(solution)/shard_map/psum | solution.py:292
  765.9 225.2 %all-reduce.53.cloned.1.call-done = (f32[1024,768]{1,0:T(8,128)}, f32[1024,768]{1,0:T(8,128)}) async-done(((f32[1024,768]{1,0:T(8,128)}, f32[1024,768]{1,0:T(8,128)}), (f32[1024,768]{1,0:T(8,128)}, f32[1024,768]{1,0:T(8,128)})) %all-reduce.53.cloned.1.call-update) | async-done | bytes 6291472 | tf_op jit(solution)/shard_map/psum | solution.py:292
  992.3 3.9 copy.420
  (687 shorter events, 162.5 us)
Async XLA Ops:
  7.2 173.5 %all-reduce.43.cloned.1.call-start = ((), (), s32[]{:S(2)}) async-start(), calls=%async_computation | async-start | bytes 524288 | tf_op jit(solution)/shard_map/psum | solution.py:221
  10.6 7.7 copy-start.1
  11.0 11.0 %copy-start.44 = (f32[128,768]{1,0:T(8,128)}, f32[128,768]{1,0:T(8,128)S(1)}, u32[]{:S(2)}) copy-start(f32[128,768]{1,0:T(8,128)S(1)} %fusion.239) | copy-start | bytes 1179652
  11.5 13.5 %copy-start.77 = (f32[128,384]{1,0:T(8,128)}, f32[128,384]{1,0:T(8,128)S(1)}, u32[]{:S(2)}) copy-start(f32[128,384]{1,0:T(8,128)S(1)} %fusion.240) | copy-start | bytes 589828
  11.5 6.8 copy-start.119
  11.5 7.3 copy-start.170
  11.5 7.4 copy-start.171
  12.3 6.7 copy-start.172
  13.4 7.9 collective-permute-start
  18.5 5.5 copy-start.150
  18.6 7.6 copy-start.106
  18.8 5.1 copy-start.138
  19.0 7.2 copy-start.115
  20.3 5.8 copy-start.117
  26.2 61.9 %copy-start.49 = (f32[6,128,64]{2,1,0:T(8,128)}, f32[6,128,64]{2,1,0:T(8,128)S(1)}, u32[]{:S(2)}) copy-start(f32[6,128,64]{2,1,0:T(8,128)S(1)} %copy.172) | copy-start | bytes 589828
  93.9 13.0 %collective-permute-start.1 = (bf16[6,128,64]{1,2,0:T(8,128)(2,1)}, bf16[6,128,64]{1,2,0:T(8,128)(2,1)}, u32[]{:S(2)}, u32[]{:S(2)}) collective-permute-start(bf16[6,128,64]{1,2,0:T(8,128)(2,1)} %convert_element_type.159), channel_id=1, source_target_pairs={{0,4},{1,5},{2,6},{3,7},{8,12},{9,13},{10,14},{11,15},{16,20},{17,... | collective-permute-start | bytes 294920 | tf_op jit(solution)/shard_map/ppermute | solution.py:15
  99.8 6.1 copy-start.11
  119.0 15.1 %copy-start.2 = (bf16[128,1024]{1,0:T(8,128)(2,1)S(1)}, bf16[128,1024]{1,0:T(8,128)(2,1)}, u32[]{:S(2)}) copy-start(bf16[128,1024]{1,0:T(8,128)(2,1)} %copy-done.1) | copy-start | bytes 786436
  119.0 15.1 %copy-start.192 = (f32[64]{0:T(128)S(1)}, f32[64]{0:T(128)}, u32[]{:S(2)}) copy-start(f32[64]{0:T(128)} %param.49) | copy-start | bytes 772
  134.1 46.5 %copy-start.4 = (bf16[128,1024]{1,0:T(8,128)(2,1)S(1)}, bf16[128,1024]{1,0:T(8,128)(2,1)}, u32[]{:S(2)}) copy-start(bf16[128,1024]{1,0:T(8,128)(2,1)} %param.36) | copy-start | bytes 786436
  134.2 47.8 %copy-start.128 = (f32[1024]{0:T(1024)S(1)}, f32[1024]{0:T(1024)}, u32[]{:S(2)}) copy-start(f32[1024]{0:T(1024)} %param.51) | copy-start | bytes 12292
  138.1 93.8 %all-reduce.45.cloned.1.call-start = ((), (), s32[]{:S(2)}) async-start(), calls=%async_computation.1 | async-start | bytes 524288 | tf_op jit(solution)/shard_map/psum | solution.py:241
  187.6 44.3 %copy-start.5 = (bf16[128,1024]{1,0:T(8,128)(2,1)S(1)}, bf16[128,1024]{1,0:T(8,128)(2,1)}, u32[]{:S(2)}) copy-start(bf16[128,1024]{1,0:T(8,128)(2,1)} %param.36) | copy-start | bytes 786436
  188.8 233.6 %all-reduce.47.cloned.1.call-start = ((), (), s32[]{:S(2)}) async-start(), calls=%async_computation.2 | async-start | bytes 190464 | tf_op jit(solution)/shard_map/psum | solution.py:292
  235.9 12.7 %copy-start.109 = (f32[128,6,64]{0,2,1:T(8,128)S(1)}, f32[128,6,64]{0,2,1:T(8,128)}, u32[]{:S(2)}) copy-start(f32[128,6,64]{0,2,1:T(8,128)} %get-tuple-element.1104) | copy-start | bytes 589828
  251.6 9.8 copy-start.104
  260.2 3.6 collective-permute-start.2
  303.1 6.3 copy-start.12
  305.1 5.5 copy-start.153
  319.6 6.4 copy-start.159
  319.6 6.4 copy-start.161
  319.6 6.4 copy-start.163
  319.6 6.4 copy-start.165
  326.9 10.3 %copy-start.151 = (f32[128,6]{0,1:T(8,128)S(1)}, f32[128,6]{0,1:T(8,128)}, u32[]{:S(2)}) copy-start(f32[128,6]{0,1:T(8,128)} %copy-done.150) | copy-start | bytes 9220
  326.9 14.4 %copy-start.3 = (bf16[128,1024]{1,0:T(8,128)(2,1)S(1)}, bf16[128,1024]{1,0:T(8,128)(2,1)}, u32[]{:S(2)}) copy-start(bf16[128,1024]{1,0:T(8,128)(2,1)} %copy-done.1) | copy-start | bytes 786436
  328.2 26.6 %copy-start.22 = (f32[128,768]{1,0:T(8,128)S(1)}, f32[128,768]{1,0:T(8,128)}, u32[]{:S(2)}) copy-start(f32[128,768]{1,0:T(8,128)} %copy-done.21) | copy-start | bytes 1179652
  328.2 26.6 %copy-start.24 = (f32[128,768]{1,0:T(8,128)S(1)}, f32[128,768]{1,0:T(8,128)}, u32[]{:S(2)}) copy-start(f32[128,768]{1,0:T(8,128)} %copy-done.23) | copy-start | bytes 1179652
  328.8 26.0 %collective-permute-start.3 = (f32[3,1920]{1,0:T(4,128)}, f32[3,1920]{1,0:T(4,128)}, u32[]{:S(2)}, u32[]{:S(2)}) collective-permute-start(f32[3,1920]{1,0:T(4,128)} %pad_maximum_fusion.4), channel_id=1, source_target_pairs={{4,0},{5,1},{6,2},{7,3},{12,8},{13,9},{14,10},{15,11},{20,16},{21,... | collective-permute-start | bytes 69128 | tf_op jit(solution)/shard_map/ppermute | solution.py:15
  341.4 13.4 %copy-start.26 = (f32[128,768]{1,0:T(8,128)S(1)}, f32[128,768]{1,0:T(8,128)}, u32[]{:S(2)}) copy-start(f32[128,768]{1,0:T(8,128)} %copy-done.25) | copy-start | bytes 1179652
  341.4 13.4 %copy-start.28 = (f32[128,768]{1,0:T(8,128)S(1)}, f32[128,768]{1,0:T(8,128)}, u32[]{:S(2)}) copy-start(f32[128,768]{1,0:T(8,128)} %copy-done.27) | copy-start | bytes 1179652
  341.4 13.4 %copy-start.30 = (f32[128,768]{1,0:T(8,128)S(1)}, f32[128,768]{1,0:T(8,128)}, u32[]{:S(2)}) copy-start(f32[128,768]{1,0:T(8,128)} %copy-done.29) | copy-start | bytes 1179652
  341.4 13.4 %copy-start.32 = (f32[128,768]{1,0:T(8,128)S(1)}, f32[128,768]{1,0:T(8,128)}, u32[]{:S(2)}) copy-start(f32[128,768]{1,0:T(8,128)} %copy-done.31) | copy-start | bytes 1179652
  366.9 163.8 %all-reduce.49.cloned.1.call-start = ((), (), s32[]{:S(2)}) async-start(), calls=%async_computation.3 | async-start | bytes 12582912 | tf_op jit(solution)/shard_map/psum | solution.py:292
  369.2 210.4 %all-reduce.57.cloned.1.call-start = ((), (), s32[]{:S(2)}) async-start(), calls=%async_computation.7 | async-start | bytes 1048576 | tf_op jit(solution)/shard_map/psum | solution.py:229
  377.1 350.5 %all-reduce.55.cloned.1.call-start = ((), (), s32[]{:S(2)}) async-start(), calls=%async_computation.6 | async-start | bytes 13369344 | tf_op jit(solution)/shard_map/psum | solution.py:296
  381.0 384.9 %all-reduce.51.cloned.1.call-start = ((), (), s32[]{:S(2)}) async-start(), calls=%async_computation.4 | async-start | bytes 190464 | tf_op jit(solution)/shard_map/psum | solution.py:292
  422.4 568.6 %all-reduce.53.cloned.1.call-start = ((), (), s32[]{:S(2)}) async-start(), calls=%async_computation.5 | async-start | bytes 12582912 | tf_op jit(solution)/shard_map/psum | solution.py:292
  530.7 48.9 %copy-start.18 = (bf16[128,1024]{1,0:T(8,128)(2,1)S(1)}, bf16[128,1024]{1,0:T(8,128)(2,1)}, u32[]{:S(2)}) copy-start(bf16[128,1024]{1,0:T(8,128)(2,1)} %all-reduce.43.cloned.1.call-done) | copy-start | bytes 786436
  (180 other events, 471.5 us)
Sparse Core Ops, SparseCore 0:
  138.2 42.3 all-reduce.42
  188.9 43.0 all-reduce.44
  367.0 55.3 all-reduce.46
  426.1 104.4 all-reduce.48
  534.1 45.5 all-reduce.56
  584.1 143.5 all-reduce.54
  730.5 35.3 all-reduce.50
  768.3 222.7 all-reduce.52
